TPU v7x, 256 devices: a whole 4x4x8 slice. The times are simulated.
256 devices in a mesh: dp: 16 (over y_lo, z), fsdp: 16 (over x, y_hi, core).
Axes of the slice: x: 4, y: 4 (y_hi: 2, y_lo: 2; y = y_hi * 2 + y_lo), z: 8, core: 2. Of those that a mesh axis runs over, the one named last changes fastest.
Arguments:
- frames: bfloat16 [256, 256, 1536], P(('dp', 'fsdp')), may hold values from -6 to 6
- cotangent: bfloat16 [256, 256, 1536], P(('dp', 'fsdp')), may hold values from -6 to 6
- lengths: int32 [256], P(('dp', 'fsdp')), may hold values from 64 to 256, as said below
- weight_slots: bfloat16 [2304, 3072], P('fsdp'), may hold values from -0.15625 to 0.15625
- owner_rows: int32 [2304], replicated, may hold values from -1 to 1535, as said below
- gain_in: float32 [1536], replicated, may hold values from 0.5 to 1.5
- gain_mid: float32 [1536], replicated, may hold values from 0.5 to 1.5
- kernel: float32 [32, 1536], replicated, may hold values from -1 to 1
Outputs:
- frame_grads: bfloat16 [256, 256, 1536], P(('dp', 'fsdp'))
- weight_grads: bfloat16 [2304, 3072], P('fsdp')
- gain_in_grad: float32 [1536], replicated
- gain_mid_grad: float32 [1536], replicated
- kernel_grad: float32 [32, 1536], replicated
Inputs may be any that keep to these rules, and one draw needn't show every extreme that they name: `owner_rows`: slots o * 144 to o * 144 + 143 belong to owner o (index o of fsdp): first the rows it holds, then -1. Each of the 1536 rows is named by exactly one slot. An owner holds between 48 and 144 rows, and some owner holds exactly 144. Rows of weight_slots in slots marked -1 are not used. `lengths`: some utterance has all 256 frames in use.
All inputs are finite; a program needn't handle non-finite values.
Results may differ from a plain program's by a relative error of at most 0.02.
Values may be sent and summed in bfloat16 or wider, within the bound.
A program may use at most 192 MiB of HBM per device.

v0:
```python
import jax
import jax.numpy as jnp
from jax import lax
from jax.sharding import PartitionSpec as P

EPSILON = 1e-05


def norm_rows(values, scales):
    row_mean = jnp.mean(values, axis=-1, keepdims=True)
    centred = values - row_mean
    spread = jnp.mean(centred * centred, axis=-1, keepdims=True)
    return centred * lax.rsqrt(spread + EPSILON) * scales


def branch_tail(projected, gain_mid, kernel, frame_keep):
    features = gain_mid.shape[0]
    kernel_taps = kernel.shape[0]
    gated = (
        projected[..., :features]
        * jax.nn.sigmoid(projected[..., features:])
        * frame_keep[..., None]
    )
    length = gated.shape[1]
    left_pad = kernel_taps // 2
    padded = jnp.pad(gated, ((0, 0), (left_pad, kernel_taps - 1 - left_pad), (0, 0)))
    convolved = jnp.zeros_like(gated)
    for offset in range(kernel_taps):
        convolved = convolved + kernel[offset] * padded[:, offset : offset + length, :]
    mixed = norm_rows(convolved, gain_mid)
    return mixed * jax.nn.sigmoid(mixed) * frame_keep[..., None]


def per_device(frames, cotangent, lengths, weight_slots, owner_rows, gain_in, gain_mid, kernel):
    utterances, length, features = frames.shape
    token_rows = utterances * length
    slot_count = owner_rows.shape[0]
    valid_slot = owner_rows >= 0
    safe_rows = jnp.where(valid_slot, owner_rows, 0)
    valid_mask = valid_slot.astype(jnp.bfloat16)
    frame_keep = (jnp.arange(length)[None, :] < lengths[:, None]).astype(jnp.float32)
    frames_wide = frames.astype(jnp.float32)
    normed, head_back = jax.vjp(norm_rows, frames_wide, gain_in)
    normed_flat = normed.astype(jnp.bfloat16).reshape(token_rows, features)
    gathered = lax.all_gather(weight_slots, "fsdp", axis=0, tiled=True)
    inverse = (
        jnp.zeros((features,), jnp.int32)
        .at[jnp.where(valid_slot, owner_rows, features)]
        .set(jnp.arange(slot_count, dtype=jnp.int32), mode="drop")
    )
    weight = jnp.take(gathered, inverse, axis=0)
    projected = jnp.dot(normed_flat, weight, preferred_element_type=jnp.float32)
    projected = projected.reshape(utterances, length, 2 * features)
    cotangent_wide = cotangent.astype(jnp.float32)

    def run_tail(projected_in, mid_scales, taps_in):
        return branch_tail(projected_in, mid_scales, taps_in, frame_keep)

    branch, tail_back = jax.vjp(run_tail, projected, gain_mid, kernel)
    projected_grad, gain_mid_grad, kernel_grad = tail_back(cotangent_wide)
    grad_flat = projected_grad.astype(jnp.bfloat16).reshape(token_rows, 2 * features)
    normed_grad = lax.dot_general(
        grad_flat, weight, (((1,), (1,)), ((), ())), preferred_element_type=jnp.float32
    )
    frames_back, gain_in_grad = head_back(normed_grad.reshape(utterances, length, features))
    frame_grads = (cotangent_wide + frames_back).astype(jnp.bfloat16)
    owned_rows = lax.psum_scatter(
        lax.dot_general(
            jnp.take(normed_flat, safe_rows, axis=1) * valid_mask[None, :],
            grad_flat,
            (((0,), (0,)), ((), ())),
            preferred_element_type=jnp.float32,
        ).astype(jnp.bfloat16),
        "fsdp",
        scatter_dimension=0,
        tiled=True,
    )
    weight_sum = lax.psum(owned_rows, "dp").astype(jnp.float32)
    gain_in_total, gain_mid_total, kernel_total = lax.psum(
        (gain_in_grad, gain_mid_grad, kernel_grad), ("dp", "fsdp")
    )
    weight_grads = weight_sum.astype(jnp.bfloat16)
    return (frame_grads, weight_grads, gain_in_total, gain_mid_total, kernel_total)


def solution(mesh):
    in_specs = (
        P(("dp", "fsdp"), None, None),
        P(("dp", "fsdp"), None, None),
        P(("dp", "fsdp")),
        P("fsdp", None),
        P(),
        P(),
        P(),
        P(),
    )
    out_specs = (P(("dp", "fsdp"), None, None), P("fsdp", None), P(), P(), P())
    return jax.shard_map(
        per_device, mesh=mesh, in_specs=in_specs, out_specs=out_specs, check_vma=False
    )
```

profile of v0, /device:TPU:2, one launch (start us, length us, event | category | flops | bytes accessed | tf_op | source)
XLA Modules:
  0.0 746.2 jit_solution(6646918404065023754)
XLA Ops:
  7.2 0.7 all-gather.2.cloned.1.call-update
  8.6 1.3 convert_reduce_fusion
  10.3 0.6 copy-done.24
  11.7 7.4 gather_fusion.1
  19.1 9.0 %scatter_custom_fusion = s32[1536]{0:T(1024)S(1)} fusion(s32[2304]{0:T(1024)S(1)} %get-tuple-element.117, s32[2304]{0:T(1024)S(1)} %iota.9, s32[]{:T(128)} %constant.48.clone.1), kind=kCustom, calls=%fused_computation.195 | custom fusion | bytes 6148 | tf_op jit(solution)/shard_map/scatter | solution.py:49
  28.7 86.9 %all-gather.2.cloned.1.call-done = bf16[2304,3072]{1,0:T(8,128)(2,1)} async-done(((bf16[144,3072]{1,0:T(8,128)(2,1)}), bf16[2304,3072]{1,0:T(8,128)(2,1)}) %all-gather.2.cloned.1.call-update) | async-done | bytes 14155792 | tf_op jit(solution)/shard_map/all_gather | solution.py:45
  115.7 24.8 %gather_fusion = bf16[1536,3072]{1,0:T(8,128)(2,1)} fusion(bf16[2304,3072]{1,0:T(8,128)(2,1)} %all-gather.2.cloned.1.call-done, s32[2048]{0:T(1024)S(1)} %pad_clamp_fusion.1), kind=kCustom, calls=%fused_computation | custom fusion | bytes 18880512 | tf_op jit(solution)/shard_map/jit(_take)/gather | solution.py:51
  140.5 6.4 convolution_bitcast_fusion
  147.3 1.2 copy-done.2
  148.6 8.2 %fusion.44 = (f32[256]{0:T(256)S(1)}, f32[1,256,1536]{2,1,0:T(8,128)S(1)}) fusion(f32[1536]{0:T(1024)S(1)} %get-tuple-element.41, f32[1536]{0:T(1024)S(1)} %get-tuple-element.71, f32[1536]{0:T(1024)S(1)} %get-tuple-element.72, f32[1536]{0:T(1024)S(1)} %get-tuple-element.42, f32[1536]{0:T(1024)S(1)} %get-tuple-element.43, f32[1536]{0:T(1024)S(1)} %get-tuple-element.44, ...), kind=kLoop, calls=%fused_computation.216 | loop fusion | flops 25165568 | bytes 3343360 | tf_op jit(solution)/shard_map/jvp()/reduce_sum | solution.py:10
  157.1 0.8 copy-done.8
  157.9 1.8 multiply_reduce_fusion.32
  159.6 0.5 fusion.42
  160.2 4.2 multiply_reduce_fusion.30
  164.4 9.1 %broadcast_multiply_fusion.31 = (f32[1,256,1536]{2,1,0:T(8,128)}, f32[1,256,1536]{2,1,0:T(8,128)}, f32[1,256,1536]{2,1,0:T(8,128)}, f32[1,256,1536]{2,1,0:T(8,12...) fusion(f32[1536]{0:T(1024)S(1)} %get-tuple-element.41, ...), kind=kLoop, calls=%fused_computation.149 | loop fusion | flops 7077888 | bytes 28417024 | tf_op jit(solution)/shard_map/transpose(jvp())/mul | solution.py:29
  173.5 7.2 broadcast_multiply_fusion
  180.7 14.8 %pad_add_fusion = f32[1,287,1536]{2,1,0:T(8,128)S(1)} fusion(f32[1,256,1536]{2,1,0:T(8,128)} %get-tuple-element.86, f32[1,256,1536]{2,1,0:T(8,128)} %get-tuple-element.87, f32[1,256,1536]{2,1,0:T(8,128)} %get-tuple-element.88, f32[1,256,1536]{2,1,0:T(8,128)} %get-tuple-element.89, f32[1,256,1536]{2,1,0:T(8,128)} %get-tuple-element.90, ...), kind=kLoop, calls=%fused_computation.24 | loop fusion | flops 11020800 | bytes 42657792 | tf_op jit(solution)/shard_map/transpose(jvp())/add_any | solution.py:29
  195.5 4.9 fusion.16
  200.9 0.8 copy-done.4
  202.1 0.5 copy-done.7
  202.6 7.9 %convolution_convert_fusion = bf16[2304,3072]{1,0:T(8,128)(2,1)} fusion(bf16[2304,256]{1,0:T(8,128)(2,1)S(1)} %copy-done.7, pred[2304]{0:T(1024)(128)(4,1)S(1)} %get-tuple-element.115, bf16[2304]{0:T(1024)(128)(2,1)S(1)} %get-tuple-element.114, f32[1,256,1536]{2,1,0:T(8,128)S(1)} %fusion.40, f32[1,256,1536]{2,1,0:T(8,128)S(1)} %get-tuple-element.75), kind=kOutput, calls=%fused_computation.3 | convolution fusion | flops 3633709056 | bytes 18488064 | tf_op jit(solution)/shard_map/dot_general | solution.py:68
  211.2 5.0 multiply_reduce_fusion.31
  216.5 1.0 pad_add_fusion.7
  217.5 8.3 %fusion.15 = (f32[256]{0:T(256)S(1)}, f32[256,1536]{1,0:T(8,128)S(1)}) fusion(bf16[1,256,1536]{2,1,0:T(8,128)(2,1)} %param.8, f32[1536]{0:T(1024)S(1)} %copy-done.12, f32[256]{0:T(256)S(1)} %copy-done.19, bf16[1536,3072]{1,0:T(8,128)(2,1)} %gather_fusion, pred[1536]{0:T(1024)(128)(4,1)S(1)} %copy-done.27, f32[1,256,1536]{2,1,0:T(8,128)} %copy-done.6, ...), kind=kOutput, calls=%fused_computation.62 | convolution fusion | flops 2424176384 | bytes 14951936 | tf_op jit(solution)/shard_map/dot_general | solution.py:62
  225.9 120.1 %reduce-scatter.2.cloned.1.call-done = bf16[144,3072]{1,0:T(8,128)(2,1)} async-done(((bf16[2304,3072]{1,0:T(8,128)(2,1)}), bf16[144,3072]{1,0:T(8,128)(2,1)}) %reduce-scatter.2.cloned.1.call-update) | async-done | bytes 884752 | tf_op jit(solution)/shard_map/reduce_scatter | solution.py:67
  346.1 0.8 fusion.10
  346.9 74.4 %all-reduce.67 = (f32[1536]{0:T(1024)}, f32[1536]{0:T(1024)}) all-reduce(f32[1536]{0:T(1024)S(1)} %get-tuple-element.39, f32[1536]{0:T(1024)S(1)} %copy-done.15), channel_id=1, replica_groups=mesh['dp'=16,'fsdp'=16] {'dp','fsdp'}, use_global_device_ids=true, to_apply=%region_12.13 | all-reduce | flops 3072 | bytes 24576 | tf_op jit(solution)/shard_map/psum | solution.py:79
  421.3 1.5 fusion.13
  422.8 175.4 %all-reduce.73.cloned.1.call-done = f32[32,1536]{1,0:T(8,128)} async-done(((f32[32,1536]{1,0:T(8,128)}), f32[32,1536]{1,0:T(8,128)}) %all-reduce.73.cloned.1.call-update) | async-done | bytes 196624 | tf_op jit(solution)/shard_map/psum | solution.py:79
  598.2 138.6 %all-reduce.71.cloned.1.call-done = bf16[144,3072]{1,0:T(8,128)(2,1)} async-done(((bf16[144,3072]{1,0:T(8,128)(2,1)}), bf16[144,3072]{1,0:T(8,128)(2,1)}) %all-reduce.71.cloned.1.call-update) | async-done | bytes 884752 | tf_op jit(solution)/shard_map/psum | solution.py:78
  736.8 2.1 copy.17
  738.9 0.7 copy.18
  (114 shorter events, 4.1 us)
Async XLA Ops:
  7.2 2.8 copy-start
  7.2 3.7 copy-start.12
  7.2 108.5 %all-gather.2.cloned.1.call-start = ((), (), s32[]{:S(2)}) async-start(), calls=%async_computation.1 | async-start | bytes 15040512 | tf_op jit(solution)/shard_map/all_gather | solution.py:45
  7.9 338.1 %reduce-scatter.2.cloned.1.call-start = ((), (), s32[]{:S(2)}) async-start(), calls=%async_computation.2 | async-start | bytes 15040512 | tf_op jit(solution)/shard_map/reduce_scatter | solution.py:67
  10.0 1.6 copy-start.18
  10.3 0.6 copy-start.24
  10.9 0.6 copy-start.20
  10.9 0.7 copy-start.13
  11.7 16.5 %copy-start.11 = (f32[32,1536]{1,0:T(8,128)S(1)}, f32[32,1536]{1,0:T(8,128)}, u32[]{:S(2)}) copy-start(f32[32,1536]{1,0:T(8,128)} %param.15) | copy-start | bytes 589828
  28.1 129.0 %copy-start.22 = (f32[256]{0:T(256)}, f32[256]{0:T(256)S(1)}, u32[]{:S(2)}) copy-start(f32[256]{0:T(256)S(1)} %compare_convert_fusion.1) | copy-start | bytes 3076
  28.7 111.8 %copy-start.26 = (pred[1536]{0:T(1024)(128)(4,1)}, pred[1536]{0:T(1024)(128)(4,1)S(1)}, u32[]{:S(2)}) copy-start(pred[1536]{0:T(1024)(128)(4,1)S(1)} %compare_and_fusion.1) | copy-start | bytes 4612
  146.9 1.7 copy-start.2
  156.7 1.1 copy-start.8
  156.7 1.1 copy-start.14
  160.2 13.3 %copy-start.16 = (f32[256]{0:T(256)}, f32[256]{0:T(256)S(1)}, u32[]{:S(2)}) copy-start(f32[256]{0:T(256)S(1)} %negate_multiply_fusion.1) | copy-start | bytes 3076
  180.7 14.8 %copy-start.3 = (f32[1,256,3072]{2,1,0:T(8,128)S(1)}, f32[1,256,3072]{2,1,0:T(8,128)}, u32[]{:S(2)}) copy-start(f32[1,256,3072]{2,1,0:T(8,128)} %copy-done.2) | copy-start | bytes 9437188
  180.7 14.8 %copy-start.5 = (f32[1,256,1536]{2,1,0:T(8,128)S(1)}, f32[1,256,1536]{2,1,0:T(8,128)}, u32[]{:S(2)}) copy-start(f32[1,256,1536]{2,1,0:T(8,128)} %get-tuple-element.85) | copy-start | bytes 4718596
  180.7 14.8 %copy-start.23 = (f32[256]{0:T(256)S(1)}, f32[256]{0:T(256)}, u32[]{:S(2)}) copy-start(f32[256]{0:T(256)} %copy-done.22) | copy-start | bytes 3076
  200.4 1.2 copy-start.4
  200.5 2.1 copy-start.7
  200.9 1.2 copy-start.6
  210.5 0.7 copy-start.17
  210.6 387.6 %all-reduce.73.cloned.1.call-start = ((), (), s32[]{:S(2)}) async-start(), calls=%async_computation.4 | async-start | bytes 393216 | tf_op jit(solution)/shard_map/psum | solution.py:79
  211.2 6.3 copy-start.19
  211.2 6.3 copy-start.27
  217.5 8.4 %copy-start.25 = (f32[256]{0:T(256)S(1)}, f32[256]{0:T(256)}, u32[]{:S(2)}) copy-start(f32[256]{0:T(256)} %copy-done.24) | copy-start | bytes 3076
  217.5 128.5 %copy-start.21 = (f32[256]{0:T(256)S(1)}, f32[256]{0:T(256)}, u32[]{:S(2)}) copy-start(f32[256]{0:T(256)} %copy-done.20) | copy-start | bytes 3076
  225.8 120.2 %copy-start.1 = (bf16[1,256,1536]{2,1,0:T(8,128)(2,1)S(1)}, bf16[1,256,1536]{2,1,0:T(8,128)(2,1)}, u32[]{:S(2)}) copy-start(bf16[1,256,1536]{2,1,0:T(8,128)(2,1)} %param.8) | copy-start | bytes 2359300
  225.9 510.9 %all-reduce.71.cloned.1.call-start = ((), (), s32[]{:S(2)}) async-start(), calls=%async_computation.3 | async-start | bytes 1769472 | tf_op jit(solution)/shard_map/psum | solution.py:78
  346.0 0.8 copy-start.15
  346.0 75.3 %copy-start.9 = (bf16[1,256,1536]{2,1,0:T(8,128)(2,1)S(1)}, bf16[1,256,1536]{2,1,0:T(8,128)(2,1)}, u32[]{:S(2)}) copy-start(bf16[1,256,1536]{2,1,0:T(8,128)(2,1)} %param.9) | copy-start | bytes 2359300
  598.2 140.8 %copy-start.10 = (f32[32,1536]{1,0:T(8,128)S(1)}, f32[32,1536]{1,0:T(8,128)}, u32[]{:S(2)}) copy-start(f32[32,1536]{1,0:T(8,128)} %all-reduce.73.cloned.1.call-done) | copy-start | bytes 589828
Sparse Core Ops, SparseCore 0:
  10.7 104.8 all-gather.1
  210.7 135.3 reduce-scatter.1
  353.0 245.1 all-reduce.72
  600.9 135.8 all-reduce.70
where the time goes:
time: 747 us; the launch traced here: 746 us
  waiting for transfers between devices  522 us (70%)
  blocking collectives  74.4 us (10%)
  other arithmetic  62.2 us (8%)
  local copies, waits for them, and re-layouts  49.9 us (7%)
  matrix products  22.6 us (3%)
  between operations  15.1 us (2%)
    psum x1, waiting for transfers between devices, per_device(): lax.psum((gain_in_grad, gain_mid_grad, kernel_grad), ('dp', 'fsdp'))  175 us
    psum x1, waiting for transfers between devices, per_device(): weight_sum = lax.psum(owned_rows, 'dp').astype(jnp.float32)  139 us
    reduce_scatter x1, waiting for transfers between devices, per_device(): lax.psum_scatter(lax.dot_general(jnp.take(normed_flat, safe_rows, axis=1)...  120 us
    all_gather x1, waiting for transfers between devices, per_device(): gathered = lax.all_gather(weight_slots, 'fsdp', axis=0, tiled=True)  86.9 us
    psum x1, blocking collectives, per_device(): lax.psum((gain_in_grad, gain_mid_grad, kernel_grad), ('dp', 'fsdp'))  74.4 us
    gather x1, local copies, waits for them, and re-layouts, per_device(): weight = jnp.take(gathered, inverse, axis=0)  24.8 us
    mul x2, other arithmetic, branch_tail(): kernel[offset] * padded[:, offset:offset + length, :]  16.3 us
  transfers between devices with their start and end apart: 4, of which 4 were waited for; matrix products, arithmetic and copies ran while one was open for 5% of the time, Pallas kernels for 0%

commit v1 on v0

--- a/solution.py
+++ b/solution.py
@@ -42,7 +42,9 @@
     frames_wide = frames.astype(jnp.float32)
     normed, head_back = jax.vjp(norm_rows, frames_wide, gain_in)
     normed_flat = normed.astype(jnp.bfloat16).reshape(token_rows, features)
-    gathered = lax.all_gather(weight_slots, "fsdp", axis=0, tiled=True)
+    gathered = jnp.concatenate(
+        lax.all_to_all(jnp.stack([weight_slots] * lax.axis_size("fsdp")), "fsdp", 0, 0), axis=0
+    )
     inverse = (
         jnp.zeros((features,), jnp.int32)
         .at[jnp.where(valid_slot, owner_rows, features)]

time: 747 us -> 776 us (1.039)
  waiting for transfers between devices: 522 us -> 534 us
  local copies, waits for them, and re-layouts: 49.9 us -> 58.4 us
    all_to_all x0 -> x1, waiting for transfers between devices: none -> 158 us  [per_device(): lax.all_to_all(jnp.stack([weight_slots] * lax.axis_size('fsdp')), 'fsdp',...]
    psum x1, waiting for transfers between devices: 175 us -> 63.5 us  [per_device(): lax.psum((gain_in_grad, gain_mid_grad, kernel_grad), ('dp', 'fsdp'))]
    all_gather x1 -> x0, waiting for transfers between devices: 86.9 us -> none  [per_device(): gathered = lax.all_gather(weight_slots, 'fsdp', axis=0, tiled=True)]
    reduce_scatter x1, waiting for transfers between devices: 120 us -> 174 us  [per_device(): lax.psum_scatter(lax.dot_general(jnp.take(normed_flat, safe_rows, axis=1)...]
    another operation x0 -> x1, local copies, waits for them, and re-layouts: none -> 8.1 us  [per_device(): jnp.stack([weight_slots] * lax.axis_size('fsdp'))]
  transfers between devices with their start and end apart: 4 -> 4, of which waited for: 4 -> 4; matrix products, arithmetic and copies ran while one was open for 5% -> 4% of each run, Pallas kernels for 0% -> 0%
where the time goes in v1:
time: 776 us
  waiting for transfers between devices  534 us (69%)
  blocking collectives  74.5 us (10%)
  other arithmetic  62.2 us (8%)
  local copies, waits for them, and re-layouts  58.4 us (8%)
  matrix products  21.9 us (3%)
  between operations  16.8 us (2%)
    reduce_scatter x1, waiting for transfers between devices, per_device(): lax.psum_scatter(lax.dot_general(jnp.take(normed_flat, safe_rows, axis=1)...  174 us
    all_to_all x1, waiting for transfers between devices, per_device(): lax.all_to_all(jnp.stack([weight_slots] * lax.axis_size('fsdp')), 'fsdp',...  158 us
    psum x1, waiting for transfers between devices, per_device(): weight_sum = lax.psum(owned_rows, 'dp').astype(jnp.float32)  139 us
    psum x1, blocking collectives, per_device(): lax.psum((gain_in_grad, gain_mid_grad, kernel_grad), ('dp', 'fsdp'))  74.5 us
    psum x1, waiting for transfers between devices, per_device(): lax.psum((gain_in_grad, gain_mid_grad, kernel_grad), ('dp', 'fsdp'))  63.5 us
    gather x1, local copies, waits for them, and re-layouts, per_device(): weight = jnp.take(gathered, inverse, axis=0)  24.8 us
    mul x2, other arithmetic, branch_tail(): kernel[offset] * padded[:, offset:offset + length, :]  17 us
  transfers between devices with their start and end apart: 4, of which 4 were waited for; matrix products, arithmetic and copies ran while one was open for 4% of the time, Pallas kernels for 0%

profile of v1, /device:TPU:2, one launch (start us, length us, event | category | flops | bytes accessed | tf_op | source)
XLA Modules:
  0.0 775.7 jit_solution(12847037711735757416)
XLA Ops:
  8.0 8.1 %stack.2 = bf16[16,144,3072]{2,1,0:T(8,128)(2,1)} broadcast(bf16[144,3072]{1,0:T(8,128)(2,1)} %param.11), dimensions={1,2} | broadcast | bytes 15040512 | tf_op jit(solution)/shard_map/stack | solution.py:46
  16.1 7.6 all-to-all-start
  25.0 0.6 copy-done.23
  26.5 7.4 gather_fusion.1
  33.9 9.0 %scatter_custom_fusion = s32[1536]{0:T(1024)S(1)} fusion(s32[2304]{0:T(1024)S(1)} %get-tuple-element.117, s32[2304]{0:T(1024)S(1)} %iota.9, s32[]{:T(128)} %constant.48.clone.1), kind=kCustom, calls=%fused_computation.195 | custom fusion | bytes 6148 | tf_op jit(solution)/shard_map/scatter | solution.py:51
  43.5 0.6 compare_convert_fusion
  44.1 158.0 %all-to-all-done = bf16[16,144,3072]{2,1,0:T(8,128)(2,1)} async-done(((bf16[16,144,3072]{2,1,0:T(8,128)(2,1)}), bf16[16,144,3072]{2,1,0:T(8,128)(2,1)}, u32[]{:S(2)}, u32[]{:S(2)}) %all-to-all-start) | async-done | bytes 14155808 | tf_op jit(solution)/shard_map/all_to_all | solution.py:46
  202.2 24.8 %gather_fusion = bf16[1536,3072]{1,0:T(8,128)(2,1)} fusion(bf16[2304,3072]{1,0:T(8,128)(2,1)} %bitcast.1, s32[2048]{0:T(1024)S(1)} %pad_clamp_fusion.1), kind=kCustom, calls=%fused_computation | custom fusion | bytes 18880512 | tf_op jit(solution)/shard_map/jit(_take)/gather | solution.py:53
  227.0 6.4 convolution_bitcast_fusion
  233.8 1.2 copy-done.2
  235.0 8.1 %fusion.44 = (f32[256]{0:T(256)S(1)}, f32[1,256,1536]{2,1,0:T(8,128)S(1)}) fusion(f32[1536]{0:T(1024)S(1)} %get-tuple-element.41, f32[1536]{0:T(1024)S(1)} %get-tuple-element.71, f32[1536]{0:T(1024)S(1)} %get-tuple-element.72, f32[1536]{0:T(1024)S(1)} %get-tuple-element.42, f32[1536]{0:T(1024)S(1)} %get-tuple-element.43, f32[1536]{0:T(1024)S(1)} %get-tuple-element.44, ...), kind=kLoop, calls=%fused_computation.216 | loop fusion | flops 25165568 | bytes 3343360 | tf_op jit(solution)/shard_map/jvp()/reduce_sum | solution.py:10
  243.5 0.8 copy-done.7
  244.3 1.2 multiply_reduce_fusion.32
  246.1 0.6 copy-done.15
  246.6 4.2 multiply_reduce_fusion.30
  250.8 9.8 %broadcast_multiply_fusion.31 = (f32[1,256,1536]{2,1,0:T(8,128)}, f32[1,256,1536]{2,1,0:T(8,128)}, f32[1,256,1536]{2,1,0:T(8,128)}, f32[1,256,1536]{2,1,0:T(8,12...) fusion(f32[1536]{0:T(1024)S(1)} %get-tuple-element.41, ...), kind=kLoop, calls=%fused_computation.149 | loop fusion | flops 7077888 | bytes 28417024 | tf_op jit(solution)/shard_map/transpose(jvp())/mul | solution.py:29
  260.7 7.2 broadcast_multiply_fusion
  267.9 14.8 %pad_add_fusion = f32[1,287,1536]{2,1,0:T(8,128)S(1)} fusion(f32[1,256,1536]{2,1,0:T(8,128)} %get-tuple-element.86, f32[1,256,1536]{2,1,0:T(8,128)} %get-tuple-element.87, f32[1,256,1536]{2,1,0:T(8,128)} %get-tuple-element.88, f32[1,256,1536]{2,1,0:T(8,128)} %get-tuple-element.89, f32[1,256,1536]{2,1,0:T(8,128)} %get-tuple-element.90, ...), kind=kLoop, calls=%fused_computation.24 | loop fusion | flops 11020800 | bytes 42657792 | tf_op jit(solution)/shard_map/transpose(jvp())/add_any | solution.py:29
  282.7 5.4 fusion.16
  288.5 0.8 copy-done.4
  290.2 7.9 %convolution_convert_fusion = bf16[2304,3072]{1,0:T(8,128)(2,1)} fusion(bf16[2304,256]{1,0:T(8,128)(2,1)S(1)} %copy-done.6, pred[2304]{0:T(1024)(128)(4,1)S(1)} %copy-done.14, bf16[2304]{0:T(1024)(128)(2,1)S(1)} %get-tuple-element.114, f32[1,256,1536]{2,1,0:T(8,128)S(1)} %fusion.40, f32[1,256,1536]{2,1,0:T(8,128)S(1)} %get-tuple-element.75), kind=kOutput, calls=%fused_computation.3 | convolution fusion | flops 3633709056 | bytes 18488064 | tf_op jit(solution)/shard_map/dot_general | solution.py:70
  298.2 5.1 multiply_reduce_fusion.31
  303.7 1.0 pad_add_fusion.7
  304.8 7.6 fusion.15
  312.5 173.9 %reduce-scatter.2.cloned.1.call-done = bf16[144,3072]{1,0:T(8,128)(2,1)} async-done(((bf16[2304,3072]{1,0:T(8,128)(2,1)}), bf16[144,3072]{1,0:T(8,128)(2,1)}) %reduce-scatter.2.cloned.1.call-update) | async-done | bytes 884752 | tf_op jit(solution)/shard_map/reduce_scatter | solution.py:69
  486.5 0.8 fusion.10
  487.2 74.5 %all-reduce.67 = (f32[1536]{0:T(1024)}, f32[1536]{0:T(1024)}) all-reduce(f32[1536]{0:T(1024)S(1)} %get-tuple-element.39, f32[1536]{0:T(1024)S(1)} %get-tuple-element.37), channel_id=1, replica_groups=mesh['dp'=16,'fsdp'=16] {'dp','fsdp'}, use_global_device_ids=true, to_apply=%region_12.13 | all-reduce | flops 3072 | bytes 24576 | tf_op jit(solution)/shard_map/psum | solution.py:81
  561.8 1.5 fusion.13
  563.2 63.5 %all-reduce.73.cloned.1.call-done = f32[32,1536]{1,0:T(8,128)} async-done(((f32[32,1536]{1,0:T(8,128)}), f32[32,1536]{1,0:T(8,128)}) %all-reduce.73.cloned.1.call-update) | async-done | bytes 196624 | tf_op jit(solution)/shard_map/psum | solution.py:81
  626.7 138.7 %all-reduce.71.cloned.1.call-done = bf16[144,3072]{1,0:T(8,128)(2,1)} async-done(((bf16[144,3072]{1,0:T(8,128)(2,1)}), bf16[144,3072]{1,0:T(8,128)(2,1)}) %all-reduce.71.cloned.1.call-update) | async-done | bytes 884752 | tf_op jit(solution)/shard_map/psum | solution.py:80
  765.4 2.1 copy.17
  767.6 0.7 copy.18
  (112 shorter events, 5.1 us)
Async XLA Ops:
  16.1 8.3 %copy-start = (bf16[1,256,1536]{2,1,0:T(8,128)(2,1)S(1)}, bf16[1,256,1536]{2,1,0:T(8,128)(2,1)}, u32[]{:S(2)}) copy-start(bf16[1,256,1536]{2,1,0:T(8,128)(2,1)} %param.8) | copy-start | bytes 2359300
  16.1 186.1 %all-to-all-start = ((bf16[16,144,3072]{2,1,0:T(8,128)(2,1)}), bf16[16,144,3072]{2,1,0:T(8,128)(2,1)}, u32[]{:S(2)}, u32[]{:S(2)}) async-start(bf16[16,144,3072]{2,1,0:T(8,128)(2,1)} %stack.2), calls=%async_computation | async-start | bytes 28311552 | tf_op jit(solution)/shard_map/all_to_all | solution.py:46
  23.7 1.9 copy-start.11
  23.7 462.7 %reduce-scatter.2.cloned.1.call-start = ((), (), s32[]{:S(2)}) async-start(), calls=%async_computation.2 | async-start | bytes 15040512 | tf_op jit(solution)/shard_map/reduce_scatter | solution.py:69
  24.6 1.3 copy-start.17
  25.0 0.6 copy-start.23
  25.6 0.6 copy-start.19
  25.6 0.9 copy-start.12
  26.5 16.5 %copy-start.10 = (f32[32,1536]{1,0:T(8,128)S(1)}, f32[32,1536]{1,0:T(8,128)}, u32[]{:S(2)}) copy-start(f32[32,1536]{1,0:T(8,128)} %param.15) | copy-start | bytes 589828
  42.9 200.6 %copy-start.21 = (f32[256]{0:T(256)}, f32[256]{0:T(256)S(1)}, u32[]{:S(2)}) copy-start(f32[256]{0:T(256)S(1)} %compare_convert_fusion.1) | copy-start | bytes 3076
  43.5 183.5 %copy-start.25 = (pred[1536]{0:T(1024)(128)(4,1)}, pred[1536]{0:T(1024)(128)(4,1)S(1)}, u32[]{:S(2)}) copy-start(pred[1536]{0:T(1024)(128)(4,1)S(1)} %compare_and_fusion.1) | copy-start | bytes 4612
  233.4 1.7 copy-start.2
  243.2 1.1 copy-start.7
  243.2 1.1 copy-start.13
  246.1 0.6 copy-start.15
  250.8 9.8 %copy-start.16 = (f32[256]{0:T(256)S(1)}, f32[256]{0:T(256)}, u32[]{:S(2)}) copy-start(f32[256]{0:T(256)} %copy-done.15) | copy-start | bytes 3076
  267.8 14.8 %copy-start.3 = (f32[1,256,3072]{2,1,0:T(8,128)S(1)}, f32[1,256,3072]{2,1,0:T(8,128)}, u32[]{:S(2)}) copy-start(f32[1,256,3072]{2,1,0:T(8,128)} %copy-done.2) | copy-start | bytes 9437188
  267.8 14.8 %copy-start.22 = (f32[256]{0:T(256)S(1)}, f32[256]{0:T(256)}, u32[]{:S(2)}) copy-start(f32[256]{0:T(256)} %copy-done.21) | copy-start | bytes 3076
  288.0 1.2 copy-start.4
  288.0 2.1 copy-start.6
  288.0 2.1 copy-start.14
  288.5 1.2 copy-start.5
  298.1 6.6 copy-start.18
  298.2 6.6 copy-start.26
  298.2 328.5 %all-reduce.73.cloned.1.call-start = ((), (), s32[]{:S(2)}) async-start(), calls=%async_computation.4 | async-start | bytes 393216 | tf_op jit(solution)/shard_map/psum | solution.py:81
  304.8 7.7 copy-start.24
  304.8 181.7 %copy-start.20 = (f32[256]{0:T(256)S(1)}, f32[256]{0:T(256)}, u32[]{:S(2)}) copy-start(f32[256]{0:T(256)} %copy-done.19) | copy-start | bytes 3076
  312.4 174.1 %copy-start.1 = (bf16[1,256,1536]{2,1,0:T(8,128)(2,1)S(1)}, bf16[1,256,1536]{2,1,0:T(8,128)(2,1)}, u32[]{:S(2)}) copy-start(bf16[1,256,1536]{2,1,0:T(8,128)(2,1)} %param.8) | copy-start | bytes 2359300
  312.4 453.0 %all-reduce.71.cloned.1.call-start = ((), (), s32[]{:S(2)}) async-start(), calls=%async_computation.3 | async-start | bytes 1769472 | tf_op jit(solution)/shard_map/psum | solution.py:80
  486.4 75.3 %copy-start.8 = (bf16[1,256,1536]{2,1,0:T(8,128)(2,1)S(1)}, bf16[1,256,1536]{2,1,0:T(8,128)(2,1)}, u32[]{:S(2)}) copy-start(bf16[1,256,1536]{2,1,0:T(8,128)(2,1)} %param.9) | copy-start | bytes 2359300
  626.7 140.8 %copy-start.9 = (f32[32,1536]{1,0:T(8,128)S(1)}, f32[32,1536]{1,0:T(8,128)}, u32[]{:S(2)}) copy-start(f32[32,1536]{1,0:T(8,128)} %all-reduce.73.cloned.1.call-done) | copy-start | bytes 589828
Sparse Core Ops, SparseCore 0:
  298.3 188.1 reduce-scatter.1
Sparse Core Ops, SparseCore 1:
  312.5 314.1 all-reduce.72
  629.4 135.9 all-reduce.70
